TPU v7x, 32 devices: a whole 2x2x4 slice. The times are simulated.
32 devices in a mesh: row: 8 (over z, y), col: 4 (over x, core).
Axes of the slice: x: 2, y: 2, z: 4, core: 2. Of those that a mesh axis runs over, the one named last changes fastest.
Arguments:
- points: bfloat16 [4096, 768], P(('row', 'col')), may hold values from -100 to 100
- labels: int32 [4096], P(('row', 'col')), may hold values from 0 to 99
- projection: bfloat16 [256, 768], replicated, may hold values from -0.015625 to 0.015625
Outputs:
- gradient: float32 [256, 768], P('row', 'col')
- class_prob: float32 [4096], P(('row', 'col'))
All inputs are finite; a program needn't handle non-finite values.
Results may differ from a plain program's by a relative error of at most 0.00081.
Values may be sent and summed in bfloat16 or wider, within the bound.
No kernel may reach another device: no remote copies, remote signals or barrier semaphores. Data moves between devices by JAX's collectives and lax.ppermute only.
A program may use at most 64 MiB of HBM per device.

v0:
```python
import jax
import jax.numpy as jnp
from jax import lax
from jax.sharding import PartitionSpec as P


def embed_rows(features, projection):
    return jnp.dot(features, projection.T, preferred_element_type=jnp.float32).astype(jnp.bfloat16)


def split_product(pull, features):
    pull_high = pull.astype(jnp.bfloat16)
    pull_low = (pull - pull_high.astype(jnp.float32)).astype(jnp.bfloat16)
    result = jnp.dot(pull_high.T, features, preferred_element_type=jnp.float32)
    return result + jnp.dot(pull_low.T, features, preferred_element_type=jnp.float32)


def shards(points, labels, projection):
    col_devs = lax.axis_size("col")
    row_devs = lax.axis_size("row")
    row_pos = lax.axis_index("row")
    col_pos = lax.axis_index("col")
    per_device = points.shape[0]
    label_wire = labels.astype(jnp.bfloat16)
    row_feat, row_lab = (
        lax.all_gather(points, "col", axis=0, tiled=True),
        lax.all_gather(label_wire, "col", axis=0, tiled=True),
    )
    col_feat, col_lab = (
        lax.all_gather(points, "row", axis=0, tiled=True),
        lax.all_gather(label_wire, "row", axis=0, tiled=True),
    )
    row_proj = embed_rows(row_feat, projection)
    col_proj = embed_rows(col_feat, projection)
    row_total = row_proj.shape[0]
    col_total = col_proj.shape[0]
    width = row_proj.shape[1]
    row_ids = row_pos * (col_devs * per_device) + jnp.arange(row_total, dtype=jnp.int32)
    col_range = jnp.arange(col_total, dtype=jnp.int32)
    col_ids = (col_range // per_device * col_devs + col_pos) * per_device + col_range % per_device
    row_norm = jnp.sum(jnp.square(row_proj.astype(jnp.float32)), axis=1)
    col_norm = jnp.sum(jnp.square(col_proj.astype(jnp.float32)), axis=1)
    blocksz = min(512, row_total)
    count = row_total // blocksz
    block_proj = row_proj.reshape(count, blocksz, width)
    block_norm = row_norm.reshape(count, blocksz)
    block_ids = row_ids.reshape(count, blocksz)
    block_lab = row_lab.reshape(count, blocksz)

    def scores(rows_proj, rows_norm, rows_ids):
        inner = jnp.dot(rows_proj, col_proj.T, preferred_element_type=jnp.float32)
        value = -(rows_norm[:, None] + col_norm[None, :] - 2.0 * inner)
        return jnp.where(rows_ids[:, None] == col_ids[None, :], -jnp.inf, value)

    def first_pass(items):
        rows_proj, rows_norm, rows_ids, rows_lab = items
        value = scores(rows_proj, rows_norm, rows_ids)
        top = jnp.max(value, axis=1)
        expo = jnp.exp(value - top[:, None])
        match = rows_lab[:, None] == col_lab[None, :]
        return (top, jnp.sum(expo, axis=1), jnp.sum(jnp.where(match, expo, 0.0), axis=1))

    local_top, local_total, local_same = lax.map(
        first_pass, (block_proj, block_norm, block_ids, block_lab)
    )
    local_top = local_top.reshape(row_total)
    local_total = local_total.reshape(row_total)
    local_same = local_same.reshape(row_total)
    top = lax.pmax(local_top, "col")
    factor = jnp.exp(local_top - top)
    total, same = lax.psum((local_total * factor, local_same * factor), "col")
    class_prob = same / total

    def second_pass(carry, items):
        col_sum, wtz = carry
        rows_proj, rows_norm, rows_ids, rows_lab, rows_top, rows_total, rows_prob = items
        value = scores(rows_proj, rows_norm, rows_ids)
        pick = jnp.exp(value - rows_top[:, None]) / rows_total[:, None]
        match = (rows_lab[:, None] == col_lab[None, :]).astype(jnp.float32)
        weight = (pick * (rows_prob[:, None] - match)).astype(jnp.bfloat16)
        weight_f = weight.astype(jnp.float32)
        row_sum = jnp.sum(weight_f, axis=1)
        pull_rows = rows_proj.astype(jnp.float32) * row_sum[:, None] - jnp.dot(
            weight, col_proj, preferred_element_type=jnp.float32
        )
        col_sum = col_sum + jnp.sum(weight_f, axis=0)
        wtz = wtz + jnp.dot(weight.T, rows_proj, preferred_element_type=jnp.float32)
        return ((col_sum, wtz), pull_rows)

    start = (jnp.zeros((col_total,), jnp.float32), jnp.zeros((col_total, width), jnp.float32))
    extras = (
        block_proj,
        block_norm,
        block_ids,
        block_lab,
        top.reshape(count, blocksz),
        total.reshape(count, blocksz),
        class_prob.reshape(count, blocksz),
    )
    (col_sum, wtz), pull_rows = lax.scan(second_pass, start, extras)
    pull_first = pull_rows.reshape(row_total, width)
    pull_second = col_proj.astype(jnp.float32) * col_sum[:, None] - wtz
    partial_value = split_product(pull_first, row_feat) + split_product(pull_second, col_feat)
    summed = lax.psum(partial_value, ("row", "col"))
    rows_each = summed.shape[0] // row_devs
    cols_each = summed.shape[1] // col_devs
    summed = lax.dynamic_slice_in_dim(summed, row_pos * rows_each, rows_each, 0)
    summed = lax.dynamic_slice_in_dim(summed, col_pos * cols_each, cols_each, 1)
    gradient = 2.0 * summed
    own_prob = lax.dynamic_slice_in_dim(class_prob, col_pos * per_device, per_device, 0)
    return (gradient, own_prob)


def solution(mesh):
    in_specs = (P(("row", "col"), None), P(("row", "col")), P())
    out_specs = (P("row", "col"), P(("row", "col")))
    return jax.shard_map(shards, mesh=mesh, in_specs=in_specs, out_specs=out_specs, check_vma=False)
```

profile of v0, /device:TPU:0, one launch (start us, length us, event | category | flops | bytes accessed | tf_op | source)
XLA Modules:
  0.0 218.3 jit_solution(3247269276336462079)
XLA Ops:
  7.2 0.7 all-gather.4.cloned.1.call-update
  8.0 0.7 convert_bitcast_fusion
  8.6 22.3 %all-gather.1 = bf16[8,1,128]{2,1,0:T(2,128)(2,1)S(1)} all-gather(bf16[1,1,128]{2,1,0:T(2,128)(2,1)S(1)} %convert_bitcast_fusion), channel_id=1, replica_groups=mesh['row'=8,'col'=4] {'row'}, dimensions={0}, use_global_device_ids=true | all-gather | bytes 2304 | tf_op jit(solution)/shard_map/all_gather | solution.py:31
  30.9 5.1 %all-gather = bf16[4,1,128]{2,1,0:T(2,128)(2,1)S(1)} all-gather(bf16[1,1,128]{2,1,0:T(2,128)(2,1)S(1)} %convert_bitcast_fusion), channel_id=1, replica_groups=mesh['row'=8,'col'=4] {'col'}, dimensions={0}, use_global_device_ids=true | all-gather | bytes 1280 | tf_op jit(solution)/shard_map/all_gather | solution.py:27
  36.0 0.6 iota_add_fusion
  36.6 8.9 %all_gather.12 = bf16[512,768]{1,0:T(8,128)(2,1)S(1)} all-gather(bf16[128,768]{1,0:T(8,128)(2,1)} %param.3), channel_id=1, replica_groups=mesh['row'=8,'col'=4] {'col'}, dimensions={0}, use_global_device_ids=true | all-gather | bytes 983040 | tf_op jit(solution)/shard_map/all_gather | solution.py:26
  45.5 1.0 fusion.7
  46.5 10.6 %all-gather.4.cloned.1.call-done = bf16[1024,768]{1,0:T(8,128)(2,1)} async-done(((bf16[128,768]{1,0:T(8,128)(2,1)}), bf16[1024,768]{1,0:T(8,128)(2,1)}) %all-gather.4.cloned.1.call-update) | async-done | bytes 1572880 | tf_op jit(solution)/shard_map/all_gather | solution.py:30
  57.1 2.0 fusion.6
  59.2 1.5 fusion.28
  60.7 5.7 %pmax.7 = f32[512]{0:T(512)S(1)} all-reduce(f32[512]{0:T(512)S(1)} %get-tuple-element.81), channel_id=1, replica_groups=mesh['row'=8,'col'=4] {'col'}, use_global_device_ids=true, to_apply=%region_3.4 | all-reduce | flops 512 | bytes 4096 | tf_op jit(solution)/shard_map/pmax | solution.py:69
  66.3 0.8 fusion.4
  67.1 0.6 fusion.26
  67.7 7.3 %all-reduce = (f32[512]{0:T(512)}, f32[512]{0:T(512)}) all-reduce(f32[512]{0:T(512)} %get-tuple-element.61, f32[512]{0:T(512)} %get-tuple-element.60), channel_id=1, replica_groups=mesh['row'=8,'col'=4] {'col'}, use_global_device_ids=true, to_apply=%region_7.8 | all-reduce | flops 1024 | bytes 8192 | tf_op jit(solution)/shard_map/psum | solution.py:71
  75.0 0.7 div.27
  75.7 1.7 convert_reduce_fusion
  77.4 0.5 convolution_subtract_fusion.1
  78.7 0.5 convolution_subtract_fusion
  79.2 0.9 copy-done.1
  80.1 0.6 fusion.9
  80.7 1.5 fusion.5
  82.2 0.6 dynamic_slice.34
  82.8 127.2 %all-reduce.3.cloned.1.call-done = f32[256,768]{1,0:T(8,128)} async-done(((f32[256,768]{1,0:T(8,128)}), f32[256,768]{1,0:T(8,128)}) %all-reduce.3.cloned.1.call-update) | async-done | bytes 786448 | tf_op jit(solution)/shard_map/psum | solution.py:104
  209.9 1.5 dynamic-slice_multiply_fusion
  (17 shorter events, 0.9 us)
Async XLA Ops:
  7.2 38.4 %copy-start = (bf16[256,768]{1,0:T(8,128)(2,1)S(1)}, bf16[256,768]{1,0:T(8,128)(2,1)}, u32[]{:S(2)}) copy-start(bf16[256,768]{1,0:T(8,128)(2,1)} %param.5) | copy-start | bytes 1179652
  7.2 49.9 %all-gather.4.cloned.1.call-start = ((), (), s32[]{:S(2)}) async-start(), calls=%async_computation | async-start | bytes 1769472 | tf_op jit(solution)/shard_map/all_gather | solution.py:30
  7.9 202.0 %all-reduce.3.cloned.1.call-start = ((), (), s32[]{:S(2)}) async-start(), calls=%async_computation.1 | async-start | bytes 1572864 | tf_op jit(solution)/shard_map/psum | solution.py:104
  57.1 2.1 copy-start.4
  59.2 1.5 copy-start.2
  75.0 2.5 %copy-start.3 = (bf16[1024,256]{0,1:T(8,128)(2,1)S(1)}, bf16[1024,256]{0,1:T(8,128)(2,1)}, u32[]{:S(2)}) copy-start(bf16[1024,256]{0,1:T(8,128)(2,1)} %copy-done.2) | copy-start | bytes 1572868
  78.7 1.4 copy-start.1
Sparse Core Ops, SparseCore 0:
  10.2 46.9 all-gather.3
  82.3 127.5 all-reduce.2
where the time goes:
time: 219 us; the launch traced here: 218 us
  waiting for transfers between devices  138 us (63%)
  blocking collectives  49.2 us (22%)
  between operations  14.2 us (6%)
  matrix products  8.26 us (4%)
  other arithmetic  6.66 us (3%)
    psum x1, waiting for transfers between devices, shards(): summed = lax.psum(partial_value, ('row', 'col'))  127 us
    all_gather x1, blocking collectives, shards(): lax.all_gather(label_wire, 'row', axis=0, tiled=True)  22.3 us
    all_gather x1, waiting for transfers between devices, shards(): lax.all_gather(points, 'row', axis=0, tiled=True)  10.6 us
    all_gather x1, blocking collectives, shards(): lax.all_gather(points, 'col', axis=0, tiled=True)  8.9 us
    psum x1, blocking collectives, shards(): total, same = lax.psum((local_total * factor, local_same * factor), 'col')  7.26 us
    pmax x1, blocking collectives, shards(): top = lax.pmax(local_top, 'col')  5.67 us
    all_gather x1, blocking collectives, shards(): lax.all_gather(label_wire, 'col', axis=0, tiled=True)  5.06 us
  transfers between devices with their start and end apart: 2, of which 2 were waited for; matrix products, arithmetic and copies ran while one was open for 1% of the time, Pallas kernels for 0%

commit v1 on v0

--- a/solution.py
+++ b/solution.py
@@ -28,7 +28,9 @@
     )
     col_feat, col_lab = (
         lax.all_gather(points, "row", axis=0, tiled=True),
-        lax.all_gather(label_wire, "row", axis=0, tiled=True),
+        jnp.concatenate(
+            lax.all_to_all(jnp.stack([label_wire] * lax.axis_size("row")), "row", 0, 0), axis=0
+        ),
     )
     row_proj = embed_rows(row_feat, projection)
     col_proj = embed_rows(col_feat, projection)

time: 219 us -> 218 us (level)
  blocking collectives: 49.2 us -> 26.8 us
  waiting for transfers between devices: 138 us -> 153 us
  starting transfers between devices: 0.08 us -> 7.38 us
    all_gather x1 -> x0, blocking collectives: 22.3 us -> none  [shards(): lax.all_gather(label_wire, 'row', axis=0, tiled=True)]
    all_gather x1, waiting for transfers between devices: 10.6 us -> 25 us  [shards(): lax.all_gather(points, 'row', axis=0, tiled=True)]
    all_to_all x0 -> x1, starting transfers between devices: none -> 7.31 us  [shards(): lax.all_to_all(jnp.stack([label_wire] * lax.axis_size('row')), 'row', 0, 0)]
  transfers between devices with their start and end apart: 2 -> 3, of which waited for: 2 -> 2; matrix products, arithmetic and copies ran while one was open for 1% -> 2% of each run, Pallas kernels for 0% -> 0%
where the time goes in v1:
time: 218 us
  waiting for transfers between devices  153 us (70%)
  blocking collectives  26.8 us (12%)
  between operations  14.2 us (7%)
  matrix products  7.59 us (3%)
  starting transfers between devices  7.38 us (3%)
  other arithmetic  6.64 us (3%)
    psum x1, waiting for transfers between devices, shards(): summed = lax.psum(partial_value, ('row', 'col'))  127 us
    all_gather x1, waiting for transfers between devices, shards(): lax.all_gather(points, 'row', axis=0, tiled=True)  25 us
    all_gather x1, blocking collectives, shards(): lax.all_gather(points, 'col', axis=0, tiled=True)  8.81 us
    all_to_all x1, starting transfers between devices, shards(): lax.all_to_all(jnp.stack([label_wire] * lax.axis_size('row')), 'row', 0, 0)  7.31 us
    psum x1, blocking collectives, shards(): total, same = lax.psum((local_total * factor, local_same * factor), 'col')  7.27 us
    pmax x1, blocking collectives, shards(): top = lax.pmax(local_top, 'col')  5.66 us
    all_gather x1, blocking collectives, shards(): lax.all_gather(label_wire, 'col', axis=0, tiled=True)  5.05 us
  transfers between devices with their start and end apart: 3, of which 2 were waited for; matrix products, arithmetic and copies ran while one was open for 2% of the time, Pallas kernels for 0%

profile of v1, /device:TPU:0, one launch (start us, length us, event | category | flops | bytes accessed | tf_op | source)
XLA Modules:
  0.0 217.7 jit_solution(2469459841967580081)
XLA Ops:
  7.2 0.7 all-gather.3.cloned.1.call-update
  7.9 0.7 convert_bitcast_fusion
  8.6 0.6 stack.2
  9.2 7.3 %all-to-all-start = ((bf16[8,1,128]{2,1,0:T(2,128)(2,1)}), bf16[8,1,128]{2,1,0:T(2,128)(2,1)S(1)}, u32[]{:S(2)}, u32[]{:S(2)}) async-start(bf16[8,1,128]{2,1,0:T(2,128)(2,1)} %stack.2), calls=%async_computation | async-start | bytes 8192 | tf_op jit(solution)/shard_map/all_to_all | solution.py:32
  16.5 8.8 %all_gather.9 = bf16[512,768]{1,0:T(8,128)(2,1)S(1)} all-gather(bf16[128,768]{1,0:T(8,128)(2,1)} %param.3), channel_id=1, replica_groups=mesh['row'=8,'col'=4] {'col'}, dimensions={0}, use_global_device_ids=true | all-gather | bytes 983040 | tf_op jit(solution)/shard_map/all_gather | solution.py:26
  25.4 1.0 fusion.7
  26.4 0.6 iota_add_fusion
  26.9 5.0 %all-gather = bf16[4,1,128]{2,1,0:T(2,128)(2,1)S(1)} all-gather(bf16[1,1,128]{2,1,0:T(2,128)(2,1)S(1)} %get-tuple-element.62), channel_id=1, replica_groups=mesh['row'=8,'col'=4] {'col'}, dimensions={0}, use_global_device_ids=true | all-gather | bytes 1280 | tf_op jit(solution)/shard_map/all_gather | solution.py:27
  32.0 25.0 %all-gather.3.cloned.1.call-done = bf16[1024,768]{1,0:T(8,128)(2,1)} async-done(((bf16[128,768]{1,0:T(8,128)(2,1)}), bf16[1024,768]{1,0:T(8,128)(2,1)}) %all-gather.3.cloned.1.call-update) | async-done | bytes 1572880 | tf_op jit(solution)/shard_map/all_gather | solution.py:30
  57.1 2.0 fusion.6
  59.1 0.8 fusion.28
  59.9 5.7 %pmax.7 = f32[512]{0:T(512)S(1)} all-reduce(f32[512]{0:T(512)S(1)} %get-tuple-element.83), channel_id=1, replica_groups=mesh['row'=8,'col'=4] {'col'}, use_global_device_ids=true, to_apply=%region_3.4 | all-reduce | flops 512 | bytes 4096 | tf_op jit(solution)/shard_map/pmax | solution.py:71
  65.6 0.8 fusion.4
  66.3 0.6 fusion.26
  66.9 7.3 %all-reduce = (f32[512]{0:T(512)}, f32[512]{0:T(512)}) all-reduce(f32[512]{0:T(512)} %get-tuple-element.61, f32[512]{0:T(512)} %get-tuple-element.60), channel_id=1, replica_groups=mesh['row'=8,'col'=4] {'col'}, use_global_device_ids=true, to_apply=%region_7.8 | all-reduce | flops 1024 | bytes 8192 | tf_op jit(solution)/shard_map/psum | solution.py:73
  74.2 0.7 div.27
  75.0 1.7 convert_reduce_fusion
  76.7 0.5 convolution_subtract_fusion.1
  78.4 0.9 copy-done.1
  79.4 0.6 fusion.9
  79.9 1.5 fusion.5
  81.5 0.6 dynamic_slice.34
  82.1 127.2 %all-reduce.3.cloned.1.call-done = f32[256,768]{1,0:T(8,128)} async-done(((f32[256,768]{1,0:T(8,128)}), f32[256,768]{1,0:T(8,128)}) %all-reduce.3.cloned.1.call-update) | async-done | bytes 786448 | tf_op jit(solution)/shard_map/psum | solution.py:106
  209.3 1.5 dynamic-slice_multiply_fusion
  (21 shorter events, 1.4 us)
Async XLA Ops:
  7.2 18.2 %copy-start = (bf16[256,768]{1,0:T(8,128)(2,1)S(1)}, bf16[256,768]{1,0:T(8,128)(2,1)}, u32[]{:S(2)}) copy-start(bf16[256,768]{1,0:T(8,128)(2,1)} %param.5) | copy-start | bytes 1179652
  7.2 49.9 %all-gather.3.cloned.1.call-start = ((), (), s32[]{:S(2)}) async-start(), calls=%async_computation.1 | async-start | bytes 1769472 | tf_op jit(solution)/shard_map/all_gather | solution.py:30
  9.2 22.8 %all-to-all-start = ((bf16[8,1,128]{2,1,0:T(2,128)(2,1)}), bf16[8,1,128]{2,1,0:T(2,128)(2,1)S(1)}, u32[]{:S(2)}, u32[]{:S(2)}) async-start(bf16[8,1,128]{2,1,0:T(2,128)(2,1)} %stack.2), calls=%async_computation | async-start | bytes 8192 | tf_op jit(solution)/shard_map/all_to_all | solution.py:32
  16.5 192.8 %all-reduce.3.cloned.1.call-start = ((), (), s32[]{:S(2)}) async-start(), calls=%async_computation.2 | async-start | bytes 1572864 | tf_op jit(solution)/shard_map/psum | solution.py:106
  57.1 2.0 copy-start.4
  57.1 2.1 copy-start.5
  59.1 0.8 copy-start.2
  74.2 2.5 %copy-start.3 = (bf16[1024,256]{0,1:T(8,128)(2,1)S(1)}, bf16[1024,256]{0,1:T(8,128)(2,1)}, u32[]{:S(2)}) copy-start(bf16[1024,256]{0,1:T(8,128)(2,1)} %copy-done.2) | copy-start | bytes 1572868
  77.9 1.4 copy-start.1
Sparse Core Ops, SparseCore 0:
  10.2 46.8 all-gather.2
  81.6 127.6 all-reduce.2
